TPU v7x, 32 devices: a whole 2x2x4 slice. The times are simulated.
32 devices in a mesh: dp: 16 (over z, y, x), tensor: 2 (over core).
Axes of the slice: x: 2, y: 2, z: 4, core: 2. Of those that a mesh axis runs over, the one named last changes fastest.
Arguments:
- acts: bfloat16 [1, 6144, 28672], P(None, 'dp', 'tensor'), may hold values from -6 to 6
- out_grads: bfloat16 [1, 6144, 8192], P(None, 'dp', 'tensor'), may hold values from -6 to 6
- proj_in: bfloat16 [1, 28672, 64], P(None, 'tensor'), may hold values from -0.03125 to 0.03125
- proj_out: bfloat16 [1, 8192, 64], P(None, 'tensor'), may hold values from -0.0625 to 0.0625
- doc_starts: int32 [64], P('dp'), may hold values from 0 to 191, as said below
- token_counts: int32 [16], P('dp'), may hold values from 192 to 384, as said below
- queries: float32 [256, 1, 4096], P('dp', None, 'tensor'), may hold values from -0.046875 to 0.046875
Outputs:
- scores: float32 [256, 64], P(None, 'dp')
- doc_grads: float32 [64, 1, 4096], P('dp', None, 'tensor')
Inputs may be any that keep to these rules, and one draw needn't show every extreme that they name: `doc_starts`: within each block of 4 entries the first is 0, the entries rise strictly, and the last is 191. `token_counts`: entry 0 equals 384.
All inputs are finite; a program needn't handle non-finite values.
Results may differ from a plain program's by a relative error of at most 0.0003.
Values sent between devices are 32-bit elements; how exact they have to be, the bound alone decides.
A program may use at most 64 MiB of HBM per device.

v0:
```python
import jax
import jax.numpy as jnp
from jax import lax
from jax.sharding import PartitionSpec as P


def document_products(member, left, right):
    spread = member[None, :, :, None] * left[:, :, None, :]
    grads = jnp.einsum("ltdr,lts->dlrs", spread, right, precision=lax.Precision.HIGHEST)
    return grads.reshape(grads.shape[0], grads.shape[1], grads.shape[2] * grads.shape[3])


def shards(acts, out_grads, proj_in, proj_out, doc_starts, token_counts, queries):
    layer_count = acts.shape[0]
    tok_rows = acts.shape[1]
    rank_size = proj_in.shape[2]
    docs_local = doc_starts.shape[0]
    left = jnp.stack([jnp.dot(acts[0], proj_in[0], preferred_element_type=jnp.float32)])
    right = jnp.stack([jnp.dot(out_grads[0], proj_out[0], preferred_element_type=jnp.float32)])
    positions = jnp.arange(tok_rows, dtype=jnp.int32)
    doc_index = jnp.sum((positions[:, None] >= doc_starts[None, :]).astype(jnp.int32), axis=1) - 1
    valid = positions < token_counts[0]
    member = (
        (doc_index[:, None] == jnp.arange(docs_local, dtype=jnp.int32)[None, :]) & valid[:, None]
    ).astype(jnp.float32)
    width = lax.axis_size("tensor")
    slot = lax.axis_index("tensor")
    share_width = rank_size * rank_size // width
    left, right = lax.psum((left, right), "tensor")
    full_grads = document_products(member, left, right)
    mine = lax.dynamic_slice_in_dim(full_grads, slot * share_width, share_width, 2)
    flat_grads = mine.reshape(docs_local, layer_count * share_width)
    piece = lax.all_gather(queries, "dp", axis=0, tiled=True)
    rows = piece.reshape(piece.shape[0], layer_count * share_width)
    partial_scores = jnp.dot(
        rows, flat_grads.T, precision=lax.Precision.HIGHEST, preferred_element_type=jnp.float32
    )
    scores = lax.psum(partial_scores, "tensor")
    return (scores, mine)


def solution(mesh):
    in_specs = (
        P(None, "dp", "tensor"),
        P(None, "dp", "tensor"),
        P(None, "tensor", None),
        P(None, "tensor", None),
        P("dp"),
        P("dp"),
        P("dp", None, "tensor"),
    )
    out_specs = (P(None, "dp"), P("dp", None, "tensor"))
    return jax.shard_map(shards, mesh=mesh, in_specs=in_specs, out_specs=out_specs, check_vma=False)
```

profile of v0, /device:TPU:0, one launch (start us, length us, event | category | flops | bytes accessed | tf_op | source)
XLA Modules:
  0.0 99.2 jit_solution(14235674293041148226)
XLA Ops:
  8.0 0.0 copy-start
  8.0 0.0 all-reduce.3.cloned.1.call-start
  8.1 0.0 copy-start.1
  8.1 8.9 %fusion = f32[384,64]{0,1:T(8,128)} fusion(bf16[1,384,14336]{2,1,0:T(8,128)(2,1)} %param.7, bf16[1,14336,64]{1,2,0:T(8,128)(2,1)} %param.9), kind=kOutput, calls=%fused_computation | convolution fusion | flops 704643072 | bytes 12943360 | tf_op jit(solution)/shard_map/dot_general | solution.py:18
  17.0 0.0 copy-done
  17.0 0.0 copy-done.1
  17.0 0.0 copy-start.2
  17.0 1.7 %fusion.2 = f32[384,64]{0,1:T(8,128)} fusion(bf16[1,384,4096]{2,1,0:T(8,128)(2,1)S(1)} %copy-done, bf16[1,4096,64]{1,2,0:T(8,128)(2,1)S(1)} %copy-done.1), kind=kOutput, calls=%fused_computation.2 | convolution fusion | flops 201326592 | bytes 3768320 | tf_op jit(solution)/shard_map/dot_general | solution.py:19
  18.7 0.0 all-reduce.3.cloned.1.call-update
  18.7 0.0 all-gather.2.cloned.1.call-start
  18.8 0.5 all-gather.2.cloned.1.call-update
  20.0 0.0 copy-done.2
  20.0 0.1 convert_reduce_fusion
  20.1 19.6 %all-reduce.3.cloned.1.call-done = (f32[384,64]{0,1:T(8,128)}, f32[384,64]{0,1:T(8,128)}) async-done(((f32[384,64]{0,1:T(8,128)}, f32[384,64]{0,1:T(8,128)}), (f32[384,64]{0,1:T(8,128)}, f32[384,64]{0,1:T(8,128)})) %all-reduce.3.cloned.1.call-update) | async-done | bytes 196624 | tf_op jit(solution)/shard_map/psum | solution.py:29
  39.7 1.8 %convolution_bitcast_fusion = f32[4,1,64,64]{2,3,0,1:T(8,128)S(1)} fusion(f32[384,64]{0,1:T(8,128)} %get-tuple-element.8, f32[384,4]{0,1:T(4,128)S(1)} %fusion.18, f32[384,64]{0,1:T(8,128)} %get-tuple-element.9), kind=kOutput, calls=%fused_computation.8 | convolution fusion | flops 75595776 | bytes 268288 | tf_op jit(solution)/shard_map/ltdr,lts->dlrs/dot_general | solution.py:9
  41.5 0.1 copy.13
  41.6 0.1 reshape.72
  41.8 0.6 copy.14
  42.4 42.8 %all-gather.2.cloned.1.call-done = f32[256,1,2048]{2,1,0:T(1,128)} async-done(((f32[16,1,2048]{2,1,0:T(1,128)}), f32[256,1,2048]{2,1,0:T(1,128)}) %all-gather.2.cloned.1.call-update) | async-done | bytes 2097168 | tf_op jit(solution)/shard_map/all_gather | solution.py:33
  85.2 3.5 %fusion.8 = f32[256,4]{0,1:T(4,128)S(1)} fusion(f32[256,1,2048]{2,1,0:T(1,128)} %all-gather.2.cloned.1.call-done, f32[4,1,2048]{2,0,1:T(4,128)S(1)} %constant_dynamic-slice_fusion), kind=kOutput, calls=%fused_computation.9 | convolution fusion | flops 25165824 | bytes 2134016 | tf_op jit(solution)/shard_map/dot_general | solution.py:35
  88.7 3.1 %psum.23 = f32[256,4]{0,1:T(4,128)} all-reduce(f32[256,4]{0,1:T(4,128)S(1)} %fusion.8), channel_id=1, replica_groups=mesh['dp'=16,'tensor'=2] {'tensor'}, use_global_device_ids=true, to_apply=%region_3.0 | all-reduce | flops 1024 | bytes 8192 | tf_op jit(solution)/shard_map/psum | solution.py:38
  (4 shorter events, 0.0 us)
Async XLA Ops:
  8.0 9.0 %copy-start = (bf16[1,384,4096]{2,1,0:T(8,128)(2,1)S(1)}, bf16[1,384,4096]{2,1,0:T(8,128)(2,1)}, u32[]{:S(2)}) copy-start(bf16[1,384,4096]{2,1,0:T(8,128)(2,1)} %param.8) | copy-start | bytes 9437188
  8.0 31.7 %all-reduce.3.cloned.1.call-start = ((), (), s32[]{:S(2)}) async-start(), calls=%async_computation.1 | async-start | bytes 393216 | tf_op jit(solution)/shard_map/psum | solution.py:29
  8.1 8.9 %copy-start.1 = (bf16[1,4096,64]{1,2,0:T(8,128)(2,1)S(1)}, bf16[1,4096,64]{1,2,0:T(8,128)(2,1)}, u32[]{:S(2)}) copy-start(bf16[1,4096,64]{1,2,0:T(8,128)(2,1)} %param.10) | copy-start | bytes 1572868
  17.0 3.0 %copy-start.2 = (s32[4]{0:T(128)S(1)}, s32[4]{0:T(128)}, u32[]{:S(2)}) copy-start(s32[4]{0:T(128)} %param.11) | copy-start | bytes 52
  18.7 66.5 %all-gather.2.cloned.1.call-start = ((), (), s32[]{:S(2)}) async-start(), calls=%async_computation | async-start | bytes 2228224 | tf_op jit(solution)/shard_map/all_gather | solution.py:33
Sparse Core Ops, SparseCore 0:
  18.8 20.8 all-reduce.2
Sparse Core Ops, SparseCore 1:
  22.0 63.2 all-gather.1
where the time goes:
time: 99.4 us; the launch traced here: 99.2 us
  waiting for transfers between devices  63 us (63%)
  between operations  16.2 us (16%)
  matrix products  15.9 us (16%)
  blocking collectives  3.05 us (3%)
    all_gather x1, waiting for transfers between devices, shards(): piece = lax.all_gather(queries, 'dp', axis=0, tiled=True)  42.8 us
    psum x1, waiting for transfers between devices, shards(): left, right = lax.psum((left, right), 'tensor')  19.6 us
    dot_general x1, matrix products, shards(): jnp.dot(acts[0], proj_in[0], preferred_element_type=jnp.float32)  8.88 us
    dot_general x1, matrix products, shards(): jnp.dot(rows, flat_grads.T, precision=lax.Precision.HIGHEST, preferred_el...  3.52 us
    psum x1, blocking collectives, shards(): scores = lax.psum(partial_scores, 'tensor')  3.05 us
  transfers between devices with their start and end apart: 2, of which 2 were waited for; matrix products, arithmetic and copies ran while one was open for 3% of the time, Pallas kernels for 0%

commit v1 on v0

v1 whole, which is shorter than its diff:
```python
import functools
import math

import jax
import jax.numpy as jnp
from jax import lax
from jax.experimental import pallas as pl
from jax.experimental.pallas import tpu as pltpu
from jax.sharding import PartitionSpec as P

MESH = pl.DeviceIdType.MESH
HIGHEST = lax.Precision.HIGHEST
NT = (((1,), (1,)), ((), ()))
DOC_DIMS = (True, False, False)


class Group:
    def __init__(self, n_dp):
        plane = math.gcd(n_dp, 4)
        y = math.gcd(plane, 2)
        self.sizes = (n_dp // plane, plane // y, y)
        self.nd = math.prod(s for s, m in zip(self.sizes, DOC_DIMS) if m)
        self.nq = math.prod(s for s, m in zip(self.sizes, DOC_DIMS) if not m)

    def split(self, dp):
        z = lax.div(dp, self.sizes[1] * self.sizes[2])
        y = lax.rem(lax.div(dp, self.sizes[2]), self.sizes[1])
        x = lax.rem(dp, self.sizes[2])
        doc, query = 0, 0
        for c, s, m in zip((z, y, x), self.sizes, DOC_DIMS):
            if m:
                doc = doc * s + c
            else:
                query = query * s + c
        return doc, query

    def join(self, doc, query):
        div = (lambda a, b: a // b) if isinstance(doc, int) and isinstance(query, int) else lax.div
        rem = (lambda a, b: a % b) if isinstance(doc, int) and isinstance(query, int) else lax.rem
        coords = []
        for s, m in zip(self.sizes[::-1], DOC_DIMS[::-1]):
            if m:
                coords.append(rem(doc, s))
                doc = div(doc, s)
            else:
                coords.append(rem(query, s))
                query = div(query, s)
        x, y, z = coords
        return (z * self.sizes[1] + y) * self.sizes[2] + x


def kernel(g, width, chunks, docs, acts, outg, pin, pout, starts, counts, queries, scores, grads,
           abuf, obuf, pbuf, rbuf, acc_l, acc_r, tbuf, xl, xr, lsum, gbuf, qbuf, part, sbuf,
           in_sems, own_sem, qs_sem, qr_sem, xs_sem, xr_sem, gs_sem, gr_sem, ss_sem, sr_sem):
    dp, me = lax.axis_index("dp"), lax.axis_index("tensor")
    doc, query = g.split(dp)
    nd, nq = g.nd, g.nq
    rank = pin.shape[0]
    rs = rank // width
    tok = acts.shape[0]
    k1, k2 = acts.shape[1] // chunks, outg.shape[1] // chunks
    qrows = queries.shape[0]
    drows = grads.shape[0]
    kkn = drows // docs
    nqr = qrows // kkn

    def at(dp_index, tensor_index):
        return {"dp": dp_index, "tensor": tensor_index}

    def turn(value, k, n):
        return lax.rem(value + k, n)

    def remote(src, dst, send, recv, to):
        return pltpu.make_async_remote_copy(
            src_ref=src, dst_ref=dst, send_sem=send, recv_sem=recv, device_id=to, device_id_type=MESH)

    reads = []
    for i in range(chunks):
        a, b = pl.ds(i * k1, k1), pl.ds(i * k2, k2)
        row = []
        for j, (src, dst, s) in enumerate(((pin, pbuf, a), (acts, abuf, a), (pout, rbuf, b), (outg, obuf, b))):
            copy = pltpu.make_async_copy(src.at[:, s], dst.at[:, s], in_sems.at[i, j])
            copy.start()
            row.append(copy)
        reads.append(row)

    barrier = pltpu.get_barrier_semaphore()
    q_peers = [turn(query, k, nq) for k in range(1, nq)]
    q_devs = [at(g.join(doc, p), me) for p in q_peers]
    t_peers = [turn(me, k, width) for k in range(1, width)]
    d_peers = [turn(doc, k, nd) for k in range(1, nd)]
    s_peers = [(turn(doc, kd, nd), turn(me, kc, width))
               for kd in range(nd) for kc in range(width) if kd or kc]
    greeted = q_devs + [at(g.join(d, query), c) for d, c in s_peers]
    for to in greeted:
        pl.semaphore_signal(barrier, inc=1, device_id=to, device_id_type=MESH)
    pl.semaphore_wait(barrier, len(greeted))

    mine = pl.ds(pl.multiple_of(query * qrows, 8), qrows)
    own = pltpu.make_async_copy(queries, qbuf.at[mine], own_sem)
    own.start()
    sends = []
    for k, to in enumerate(q_devs):
        copy = remote(queries, qbuf.at[mine], qs_sem.at[k], qr_sem.at[query], to)
        copy.start()
        sends.append(copy)

    for i in range(chunks):
        for copy in reads[i]:
            copy.wait()
        a, b = pl.ds(i * k1, k1), pl.ds(i * k2, k2)
        dl = lax.dot_general(abuf[:, a], pbuf[:, a], NT, preferred_element_type=jnp.float32)
        dr = lax.dot_general(obuf[:, b], rbuf[:, b], NT, preferred_element_type=jnp.float32)
        if i:
            dl, dr = dl + acc_l[...], dr + acc_r[...]
        if i < chunks - 1:
            acc_l[...] = dl
            acc_r[...] = dr
    tbuf[...] = jnp.concatenate([dl, dr], axis=1).T

    rights = pl.ds(rank, rank)
    for k, p in enumerate(t_peers):
        share = pl.ds(pl.multiple_of(p * rs, 8), rs)
        for j, (src, dst) in enumerate(((tbuf.at[rights], xr), (tbuf.at[share], xl))):
            copy = remote(src, dst.at[me], xs_sem.at[k, j], xr_sem.at[me, j], at(dp, p))
            copy.start()
            sends.append(copy)
    left = tbuf[pl.ds(pl.multiple_of(me * rs, 8), rs), :]
    right = tbuf[rights, :]
    for k, p in enumerate(t_peers):
        for j, dst in enumerate((xr, xl)):
            remote(dst.at[p], dst.at[p], xs_sem.at[k, j], xr_sem.at[p, j], at(dp, p)).wait_recv()
        left = left + xl[p]
        right = right + xr[p]
    tiles = tok // 128
    for i in range(tiles):
        lsum[i * rs:(i + 1) * rs, :] = left[:, i * 128:(i + 1) * 128]

    slot = lax.broadcasted_iota(jnp.int32, (1, tok), 1)
    count = counts[0]
    member = []
    for d in range(docs):
        end = count if d == docs - 1 else jnp.minimum(starts[d + 1], count)
        member.append(jnp.where((slot >= starts[d]) & (slot < end), 1.0, 0.0))
    halves = []
    for odd in range(2):
        rows = jnp.concatenate(
            [lsum[pl.ds(i * rs + odd, rs // 2, stride=2), :] for i in range(tiles)], axis=1)
        spread = jnp.concatenate([rows * m for m in member], axis=0)
        halves.append(lax.dot_general(spread, right, NT, precision=HIGHEST, preferred_element_type=jnp.float32))
    mine_grads = jnp.concatenate(halves, axis=1)
    grads[...] = mine_grads
    gmine = pl.ds(pl.multiple_of(doc * drows, 8), drows)
    gbuf[gmine, :] = mine_grads
    for k, d in enumerate(d_peers):
        copy = remote(gbuf.at[gmine], gbuf.at[gmine], gs_sem.at[k], gr_sem.at[doc], at(g.join(d, query), me))
        copy.start()
        sends.append(copy)

    own.wait()
    for k, p in enumerate(q_peers):
        there = qbuf.at[pl.ds(pl.multiple_of(p * qrows, 8), qrows)]
        remote(there, there, qs_sem.at[k], qr_sem.at[p], q_devs[k]).wait_recv()
    q = jnp.concatenate([qbuf[pl.ds(k, nq * nqr, stride=kkn), :] for k in range(kkn)], axis=1)
    for k, d in enumerate(d_peers):
        there = gbuf.at[pl.ds(pl.multiple_of(d * drows, 8), drows)]
        remote(there, there, gs_sem.at[k], gr_sem.at[d], at(g.join(d, query), me)).wait_recv()
    gr = jnp.concatenate([gbuf[pl.ds(k, nd * docs, stride=kkn), :] for k in range(kkn)], axis=1)
    s = lax.dot_general(gr, q, NT, precision=HIGHEST, preferred_element_type=jnp.float32)
    for d in range(nd):
        part[d] = s[d * docs:(d + 1) * docs, :]
    mine_slot = doc * width + me
    for k, (d, c) in enumerate(s_peers):
        copy = remote(part.at[d], sbuf.at[mine_slot], ss_sem.at[k], sr_sem.at[mine_slot], at(g.join(d, query), c))
        copy.start()
        sends.append(copy)
    sbuf[mine_slot] = part[doc]
    for k, (d, c) in enumerate(s_peers):
        there = sbuf.at[d * width + c]
        remote(there, there, ss_sem.at[k], sr_sem.at[d * width + c], at(g.join(d, query), c)).wait_recv()
    pieces = {}
    for d in range(nd):
        total = sbuf[d * width]
        for c in range(1, width):
            total = total + sbuf[d * width + c]
        for p in range(nq):
            pieces[g.join(d, p)] = total[:, p * nqr:(p + 1) * nqr]
    scores[...] = jnp.concatenate([pieces[i] for i in range(nd * nq)], axis=1)
    for copy in sends:
        copy.wait_send()


def shards(n_dp, width, acts, out_grads, proj_in, proj_out, doc_starts, token_counts, queries):
    layers, tok, f1 = acts.shape
    f2 = out_grads.shape[2]
    rank = proj_in.shape[2]
    docs = doc_starts.shape[0]
    nqr, _, share = queries.shape
    g = Group(n_dp)
    kkn = share // 128
    rs = rank // width
    chunks = math.gcd(f1 // 256, f2 // 256)
    lanes = 2 * rank
    f32, bf16 = jnp.float32, jnp.bfloat16
    dma = pltpu.SemaphoreType.DMA
    hbm = pl.BlockSpec(memory_space=pl.ANY)
    smem = pl.BlockSpec(memory_space=pltpu.SMEM)
    vmem = pl.BlockSpec(memory_space=pltpu.VMEM)
    scores, grads = pl.pallas_call(
        functools.partial(kernel, g, width, chunks, docs),
        out_shape=(jax.ShapeDtypeStruct((docs, nqr * n_dp), f32),
                   jax.ShapeDtypeStruct((docs * kkn, 128), f32)),
        in_specs=[hbm, hbm, hbm, hbm, smem, smem, hbm],
        out_specs=(vmem, vmem),
        scratch_shapes=[
            pltpu.VMEM((tok, f1), bf16),
            pltpu.VMEM((tok, f2), bf16),
            pltpu.VMEM((rank, f1), bf16),
            pltpu.VMEM((rank, f2), bf16),
            pltpu.VMEM((tok, rank), f32),
            pltpu.VMEM((tok, rank), f32),
            pltpu.VMEM((lanes, tok), f32),
            pltpu.VMEM((width, rs, tok), f32),
            pltpu.VMEM((width, rank, tok), f32),
            pltpu.VMEM((tok // 128 * rs, 128), f32),
            pltpu.VMEM((g.nd * docs * kkn, 128), f32),
            pltpu.VMEM((g.nq * nqr * kkn, 128), f32),
            pltpu.VMEM((g.nd, docs, g.nq * nqr), f32),
            pltpu.VMEM((g.nd * width, docs, g.nq * nqr), f32),
            dma((chunks, 4)), dma,
            dma((g.nq,)), dma((g.nq,)),
            dma((width, 2)), dma((width, 2)),
            dma((g.nd,)), dma((g.nd,)),
            dma((g.nd * width,)), dma((g.nd * width,)),
        ],
        compiler_params=pltpu.CompilerParams(
            collective_id=0, has_side_effects=True, vmem_limit_bytes=56 * 1024 * 1024),
    )(acts[0], out_grads[0], proj_in[0].T, proj_out[0].T, doc_starts, token_counts,
      queries.reshape(nqr * kkn, 128))
    return scores.T, grads.reshape(docs, 1, share)


def solution(mesh):
    in_specs = (
        P(None, "dp", "tensor"),
        P(None, "dp", "tensor"),
        P(None, "tensor", None),
        P(None, "tensor", None),
        P("dp"),
        P("dp"),
        P("dp", None, "tensor"),
    )
    out_specs = (P(None, "dp"), P("dp", None, "tensor"))
    body = functools.partial(shards, mesh.shape["dp"], mesh.shape["tensor"])
    return jax.shard_map(body, mesh=mesh, in_specs=in_specs, out_specs=out_specs, check_vma=False)
```

time: 99.4 us -> 29.3 us (0.29)
  waiting for transfers between devices: 63 us -> 0 us
  Pallas kernels: 0 us -> 25.1 us
  matrix products: 15.9 us -> 0 us
  between operations: 16.2 us -> 1.29 us
  blocking collectives: 3.05 us -> 0 us
  local copies, waits for them, and re-layouts: 0.88 us -> 2.65 us
    all_gather x1 -> x0, waiting for transfers between devices: 42.8 us -> none  [shards(): piece = lax.all_gather(queries, 'dp', axis=0, tiled=True)]
    pallas_call x0 -> x1, Pallas kernels: none -> 25.1 us  [shards(): pl.pallas_call(functools.partial(kernel, g, width, chunks, docs), out_sha...]
    psum x1 -> x0, waiting for transfers between devices: 19.6 us -> none  [shards(): left, right = lax.psum((left, right), 'tensor')]
    dot_general x4 -> x0, matrix products: 15.9 us -> none  [the longest x1 8.88 us: shards(): jnp.dot(acts[0], proj_in[0], preferred_element_type=jnp.float32)]
    psum x1 -> x0, blocking collectives: 3.05 us -> none  [shards(): scores = lax.psum(partial_scores, 'tensor')]
    unnamed x7 -> x2, local copies, waits for them, and re-layouts: 0.67 us -> 2.65 us
  transfers between devices with their start and end apart: 2 -> 0, of which waited for: 2 -> 0; matrix products, arithmetic and copies ran while one was open for 3% -> 0% of each run, Pallas kernels for 0% -> 0%
where the time goes in v1:
time: 29.3 us; the launch traced here: 29 us
  Pallas kernels  25.1 us (86%)
  local copies, waits for them, and re-layouts  2.65 us (9%)
  between operations  1.29 us (4%)
    pallas_call x1, Pallas kernels, shards(): pl.pallas_call(functools.partial(kernel, g, width, chunks, docs), out_sha...  25.1 us
    unnamed x2, local copies, waits for them, and re-layouts  2.65 us

profile of v1, /device:TPU:0, one launch (start us, length us, event | category | flops | bytes accessed | tf_op | source)
XLA Modules:
  0.0 29.0 jit_solution(11177599032596827203)
XLA Ops:
  1.3 25.1 %shard_map.86 = (f32[4,256]{1,0:T(4,128)}, f32[64,128]{1,0:T(8,128)}) custom-call(bf16[384,14336]{1,0:T(8,128)(2,1)} %bitcast.11, bf16[384,4096]{1,0:T(8,128)(2,1)} %bitcast.12, bf16[64,14336]{1,0:T(8,128)(2,1)} %bitcast.13, bf16[64,4096]{1,0:T(8,128)(2,1)} %bitcast.14, s32[4]{0:T(128)} %starts.1, s32[1]{0:T(128)S(6)} %copy.12.counts, f32[256,128]{1,0:T(8,128)} %bitcast.15), custom_call_target="tpu_custom_call" | custom-call | tf_op jit(solution)/shard_map/pallas_call | solution.py:209
  26.4 1.3 %copy.13 = f32[256,4]{0,1:T(4,128)} copy(f32[256,4]{0,1:T(4,128)} %bitcast.17) | data formatting | bytes 8192
  27.7 1.4 %copy.14 = f32[4,1,2048]{2,1,0:T(1,128)} copy(f32[4,1,2048]{2,1,0:T(1,128)} %bitcast.16) | data formatting | bytes 65536

commit v2 on v1

--- a/solution.py
+++ b/solution.py
@@ -9,8 +9,8 @@
 from jax.sharding import PartitionSpec as P
 
 MESH = pl.DeviceIdType.MESH
-HIGHEST = lax.Precision.HIGHEST
 NT = (((1,), (1,)), ((), ()))
+GREET_AT = 3
 DOC_DIMS = (True, False, False)
 
 
@@ -49,9 +49,21 @@
         return (z * self.sizes[1] + y) * self.sizes[2] + x
 
 
-def kernel(g, width, chunks, docs, acts, outg, pin, pout, starts, counts, queries, scores, grads,
-           abuf, obuf, pbuf, rbuf, acc_l, acc_r, tbuf, xl, xr, lsum, gbuf, qbuf, part, sbuf,
-           in_sems, own_sem, qs_sem, qr_sem, xs_sem, xr_sem, gs_sem, gr_sem, ss_sem, sr_sem):
+def split(value):
+    high = value.astype(jnp.bfloat16)
+    return high, (value - high.astype(jnp.float32)).astype(jnp.bfloat16)
+
+
+def split_dot(a, b):
+    def dot(x, y):
+        return lax.dot_general(x, y, NT, preferred_element_type=jnp.float32)
+
+    return dot(a[0], b[0]) + (dot(a[0], b[1]) + dot(a[1], b[0]))
+
+
+def kernel(g, width, chunks, docs, acts, outg, pin, pout, starts_hbm, counts_hbm, queries, scores, grads,
+           starts, counts, abuf, obuf, pbuf, rbuf, acc_l, acc_r, tbuf, xl, xr, lsum, gbuf, qbuf, qhl, part, sbuf,
+           in_sems, own_sem, bound_sem, qs_sem, qr_sem, xs_sem, xr_sem, gs_sem, gr_sem, ss_sem, sr_sem):
     dp, me = lax.axis_index("dp"), lax.axis_index("tensor")
     doc, query = g.split(dp)
     nd, nq = g.nd, g.nq
@@ -74,6 +86,10 @@
         return pltpu.make_async_remote_copy(
             src_ref=src, dst_ref=dst, send_sem=send, recv_sem=recv, device_id=to, device_id_type=MESH)
 
+    mine = pl.ds(pl.multiple_of(query * qrows, 8), qrows)
+    own = pltpu.make_async_copy(queries, qbuf.at[mine], own_sem)
+    bounds = [pltpu.make_async_copy(starts_hbm, starts, bound_sem.at[0]),
+              pltpu.make_async_copy(counts_hbm, counts, bound_sem.at[1])]
     reads = []
     for i in range(chunks):
         a, b = pl.ds(i * k1, k1), pl.ds(i * k2, k2)
@@ -94,29 +110,31 @@
     greeted = q_devs + [at(g.join(d, query), c) for d, c in s_peers]
     for to in greeted:
         pl.semaphore_signal(barrier, inc=1, device_id=to, device_id_type=MESH)
-    pl.semaphore_wait(barrier, len(greeted))
-
-    mine = pl.ds(pl.multiple_of(query * qrows, 8), qrows)
-    own = pltpu.make_async_copy(queries, qbuf.at[mine], own_sem)
-    own.start()
     sends = []
-    for k, to in enumerate(q_devs):
-        copy = remote(queries, qbuf.at[mine], qs_sem.at[k], qr_sem.at[query], to)
-        copy.start()
-        sends.append(copy)
 
     for i in range(chunks):
+        if i == min(GREET_AT, chunks - 1):
+            pl.semaphore_wait(barrier, len(greeted))
+
+            own.start()
+            for copy in bounds:
+                copy.start()
+            for k, to in enumerate(q_devs):
+                copy = remote(queries, qbuf.at[mine], qs_sem.at[k], qr_sem.at[query], to)
+                copy.start()
+                sends.append(copy)
         for copy in reads[i]:
             copy.wait()
         a, b = pl.ds(i * k1, k1), pl.ds(i * k2, k2)
-        dl = lax.dot_general(abuf[:, a], pbuf[:, a], NT, preferred_element_type=jnp.float32)
-        dr = lax.dot_general(obuf[:, b], rbuf[:, b], NT, preferred_element_type=jnp.float32)
+        dl = lax.dot_general(pbuf[:, a], abuf[:, a], NT, preferred_element_type=jnp.float32)
+        dr = lax.dot_general(rbuf[:, b], obuf[:, b], NT, preferred_element_type=jnp.float32)
         if i:
             dl, dr = dl + acc_l[...], dr + acc_r[...]
         if i < chunks - 1:
             acc_l[...] = dl
             acc_r[...] = dr
-    tbuf[...] = jnp.concatenate([dl, dr], axis=1).T
+    tbuf[:rank, :] = dl
+    tbuf[rank:, :] = dr
 
     rights = pl.ds(rank, rank)
     for k, p in enumerate(t_peers):
@@ -136,6 +154,8 @@
     for i in range(tiles):
         lsum[i * rs:(i + 1) * rs, :] = left[:, i * 128:(i + 1) * 128]
 
+    for copy in bounds:
+        copy.wait()
     slot = lax.broadcasted_iota(jnp.int32, (1, tok), 1)
     count = counts[0]
     member = []
@@ -147,8 +167,9 @@
         rows = jnp.concatenate(
             [lsum[pl.ds(i * rs + odd, rs // 2, stride=2), :] for i in range(tiles)], axis=1)
         spread = jnp.concatenate([rows * m for m in member], axis=0)
-        halves.append(lax.dot_general(spread, right, NT, precision=HIGHEST, preferred_element_type=jnp.float32))
-    mine_grads = jnp.concatenate(halves, axis=1)
+        halves.append(spread)
+    prod = split_dot(split(jnp.concatenate(halves, axis=0)), split(right))
+    mine_grads = jnp.concatenate([prod[:drows], prod[drows:]], axis=1)
     grads[...] = mine_grads
     gmine = pl.ds(pl.multiple_of(doc * drows, 8), drows)
     gbuf[gmine, :] = mine_grads
@@ -161,12 +182,15 @@
     for k, p in enumerate(q_peers):
         there = qbuf.at[pl.ds(pl.multiple_of(p * qrows, 8), qrows)]
         remote(there, there, qs_sem.at[k], qr_sem.at[p], q_devs[k]).wait_recv()
-    q = jnp.concatenate([qbuf[pl.ds(k, nq * nqr, stride=kkn), :] for k in range(kkn)], axis=1)
+    for k in range(kkn):
+        high, low = split(qbuf[pl.ds(k, nq * nqr, stride=kkn), :])
+        qhl[:nq * nqr, k * 128:(k + 1) * 128] = high
+        qhl[nq * nqr:, k * 128:(k + 1) * 128] = low
     for k, d in enumerate(d_peers):
         there = gbuf.at[pl.ds(pl.multiple_of(d * drows, 8), drows)]
         remote(there, there, gs_sem.at[k], gr_sem.at[d], at(g.join(d, query), me)).wait_recv()
     gr = jnp.concatenate([gbuf[pl.ds(k, nd * docs, stride=kkn), :] for k in range(kkn)], axis=1)
-    s = lax.dot_general(gr, q, NT, precision=HIGHEST, preferred_element_type=jnp.float32)
+    s = split_dot(split(gr), (qhl[:nq * nqr, :], qhl[nq * nqr:, :]))
     for d in range(nd):
         part[d] = s[d * docs:(d + 1) * docs, :]
     mine_slot = doc * width + me
@@ -190,6 +214,11 @@
         copy.wait_send()
 
 
+def finish(scores, grads, scores_out, grads_out):
+    scores_out[...] = scores[...]
+    grads_out[...] = grads[...]
+
+
 def shards(n_dp, width, acts, out_grads, proj_in, proj_out, doc_starts, token_counts, queries):
     layers, tok, f1 = acts.shape
     f2 = out_grads.shape[2]
@@ -204,30 +233,32 @@
     f32, bf16 = jnp.float32, jnp.bfloat16
     dma = pltpu.SemaphoreType.DMA
     hbm = pl.BlockSpec(memory_space=pl.ANY)
-    smem = pl.BlockSpec(memory_space=pltpu.SMEM)
     vmem = pl.BlockSpec(memory_space=pltpu.VMEM)
     scores, grads = pl.pallas_call(
         functools.partial(kernel, g, width, chunks, docs),
         out_shape=(jax.ShapeDtypeStruct((docs, nqr * n_dp), f32),
                    jax.ShapeDtypeStruct((docs * kkn, 128), f32)),
-        in_specs=[hbm, hbm, hbm, hbm, smem, smem, hbm],
+        in_specs=[hbm] * 7,
         out_specs=(vmem, vmem),
         scratch_shapes=[
+            pltpu.SMEM((docs,), jnp.int32),
+            pltpu.SMEM((1,), jnp.int32),
             pltpu.VMEM((tok, f1), bf16),
             pltpu.VMEM((tok, f2), bf16),
             pltpu.VMEM((rank, f1), bf16),
             pltpu.VMEM((rank, f2), bf16),
-            pltpu.VMEM((tok, rank), f32),
-            pltpu.VMEM((tok, rank), f32),
+            pltpu.VMEM((rank, tok), f32),
+            pltpu.VMEM((rank, tok), f32),
             pltpu.VMEM((lanes, tok), f32),
             pltpu.VMEM((width, rs, tok), f32),
             pltpu.VMEM((width, rank, tok), f32),
             pltpu.VMEM((tok // 128 * rs, 128), f32),
             pltpu.VMEM((g.nd * docs * kkn, 128), f32),
             pltpu.VMEM((g.nq * nqr * kkn, 128), f32),
+            pltpu.VMEM((2 * g.nq * nqr, share), bf16),
             pltpu.VMEM((g.nd, docs, g.nq * nqr), f32),
             pltpu.VMEM((g.nd * width, docs, g.nq * nqr), f32),
-            dma((chunks, 4)), dma,
+            dma((chunks, 4)), dma, dma((2,)),
             dma((g.nq,)), dma((g.nq,)),
             dma((width, 2)), dma((width, 2)),
             dma((g.nd,)), dma((g.nd,)),
@@ -237,6 +268,12 @@
             collective_id=0, has_side_effects=True, vmem_limit_bytes=56 * 1024 * 1024),
     )(acts[0], out_grads[0], proj_in[0].T, proj_out[0].T, doc_starts, token_counts,
       queries.reshape(nqr * kkn, 128))
+    scores, grads = pl.pallas_call(
+        finish,
+        out_shape=(jax.ShapeDtypeStruct(scores.shape, f32), jax.ShapeDtypeStruct(grads.shape, f32)),
+        in_specs=[vmem, vmem],
+        out_specs=(vmem, vmem),
+    )(scores, grads)
     return scores.T, grads.reshape(docs, 1, share)
 
 

time: 29.3 us -> 23.6 us (0.81)
  Pallas kernels: 25.1 us -> 22.1 us
  local copies, waits for them, and re-layouts: 2.65 us -> 0 us
    pallas_call x1, Pallas kernels: 25.1 us -> 20.7 us  [shards(): pl.pallas_call(functools.partial(kernel, g, width, chunks, docs), out_sha...]
    unnamed x2 -> x0, local copies, waits for them, and re-layouts: 2.65 us -> none
    pallas_call x0 -> x1, Pallas kernels: none -> 1.38 us  [shards(): pl.pallas_call(finish, out_shape=(jax.ShapeDtypeStruct(scores.shape, f32)...]
where the time goes in v2:
time: 23.6 us; the launch traced here: 23.4 us
  Pallas kernels  22.1 us (94%)
  between operations  1.29 us (5%)
    pallas_call x1, Pallas kernels, shards(): pl.pallas_call(functools.partial(kernel, g, width, chunks, docs), out_sha...  20.7 us
    pallas_call x1, Pallas kernels, shards(): pl.pallas_call(finish, out_shape=(jax.ShapeDtypeStruct(scores.shape, f32)...  1.38 us

profile of v2, /device:TPU:0, one launch (start us, length us, event | category | flops | bytes accessed | tf_op | source)
XLA Modules:
  0.0 23.4 jit_solution(7374991278182332762)
XLA Ops:
  1.3 20.7 %shard_map.86 = (f32[4,256]{1,0:T(4,128)}, f32[64,128]{1,0:T(8,128)}) custom-call(bf16[384,14336]{1,0:T(8,128)(2,1)} %bitcast.11, bf16[384,4096]{1,0:T(8,128)(2,1)} %bitcast.12, bf16[64,14336]{1,0:T(8,128)(2,1)} %bitcast.13, bf16[64,4096]{1,0:T(8,128)(2,1)} %bitcast.14, s32[4]{0:T(128)} %starts_hbm.1, s32[1]{0:T(128)S(6)} %copy.10.counts_hbm, ...), custom_call_target="tpu_custom_call" | custom-call | tf_op jit(solution)/shard_map/pallas_call | solution.py:237
  22.0 1.4 %shard_map.87 = (f32[4,256]{1,0:T(4,128)}, f32[64,128]{1,0:T(8,128)}) custom-call(f32[4,256]{1,0:T(4,128)} %get-tuple-element.6.scores, f32[64,128]{1,0:T(8,128)} %get-tuple-element.7.grads), custom_call_target="tpu_custom_call" | custom-call | tf_op jit(solution)/shard_map/pallas_call | solution.py:271

commit v3 on v2

--- a/solution.py
+++ b/solution.py
@@ -47,6 +47,15 @@
                 query = div(query, s)
         x, y, z = coords
         return (z * self.sizes[1] + y) * self.sizes[2] + x
+
+
+def far_first(place, n):
+    low, high, order = 0, n - 1, []
+    for _ in range(n - 1):
+        down = place - low >= high - place
+        order.append(jnp.where(down, low, high))
+        low, high = jnp.where(down, low + 1, low), jnp.where(down, high, high - 1)
+    return order
 
 
 def split(value):
@@ -104,9 +113,8 @@
     q_peers = [turn(query, k, nq) for k in range(1, nq)]
     q_devs = [at(g.join(doc, p), me) for p in q_peers]
     t_peers = [turn(me, k, width) for k in range(1, width)]
-    d_peers = [turn(doc, k, nd) for k in range(1, nd)]
-    s_peers = [(turn(doc, kd, nd), turn(me, kc, width))
-               for kd in range(nd) for kc in range(width) if kd or kc]
+    d_peers = far_first(doc, nd)
+    s_peers = [(d, turn(me, kc, width)) for d in d_peers for kc in range(width)] + [(doc, c) for c in t_peers]
     greeted = q_devs + [at(g.join(d, query), c) for d, c in s_peers]
     for to in greeted:
         pl.semaphore_signal(barrier, inc=1, device_id=to, device_id_type=MESH)
@@ -143,6 +151,14 @@
             copy = remote(src, dst.at[me], xs_sem.at[k, j], xr_sem.at[me, j], at(dp, p))
             copy.start()
             sends.append(copy)
+    for copy in bounds:
+        copy.wait()
+    slot = lax.broadcasted_iota(jnp.int32, (1, tok), 1)
+    count = counts[0]
+    member = []
+    for d in range(docs):
+        end = count if d == docs - 1 else jnp.minimum(starts[d + 1], count)
+        member.append(jnp.where((slot >= starts[d]) & (slot < end), 1.0, 0.0))
     left = tbuf[pl.ds(pl.multiple_of(me * rs, 8), rs), :]
     right = tbuf[rights, :]
     for k, p in enumerate(t_peers):
@@ -154,14 +170,6 @@
     for i in range(tiles):
         lsum[i * rs:(i + 1) * rs, :] = left[:, i * 128:(i + 1) * 128]
 
-    for copy in bounds:
-        copy.wait()
-    slot = lax.broadcasted_iota(jnp.int32, (1, tok), 1)
-    count = counts[0]
-    member = []
-    for d in range(docs):
-        end = count if d == docs - 1 else jnp.minimum(starts[d + 1], count)
-        member.append(jnp.where((slot >= starts[d]) & (slot < end), 1.0, 0.0))
     halves = []
     for odd in range(2):
         rows = jnp.concatenate(
@@ -214,11 +222,6 @@
         copy.wait_send()
 
 
-def finish(scores, grads, scores_out, grads_out):
-    scores_out[...] = scores[...]
-    grads_out[...] = grads[...]
-
-
 def shards(n_dp, width, acts, out_grads, proj_in, proj_out, doc_starts, token_counts, queries):
     layers, tok, f1 = acts.shape
     f2 = out_grads.shape[2]
@@ -232,12 +235,11 @@
     lanes = 2 * rank
     f32, bf16 = jnp.float32, jnp.bfloat16
     dma = pltpu.SemaphoreType.DMA
-    hbm = pl.BlockSpec(memory_space=pl.ANY)
+    hbm = pl.BlockSpec(memory_space=pltpu.HBM)
     vmem = pl.BlockSpec(memory_space=pltpu.VMEM)
     scores, grads = pl.pallas_call(
         functools.partial(kernel, g, width, chunks, docs),
-        out_shape=(jax.ShapeDtypeStruct((docs, nqr * n_dp), f32),
-                   jax.ShapeDtypeStruct((docs * kkn, 128), f32)),
+        out_shape=(pltpu.VMEM((docs, nqr * n_dp), f32), pltpu.VMEM((docs * kkn, 128), f32)),
         in_specs=[hbm] * 7,
         out_specs=(vmem, vmem),
         scratch_shapes=[
@@ -268,12 +270,6 @@
             collective_id=0, has_side_effects=True, vmem_limit_bytes=56 * 1024 * 1024),
     )(acts[0], out_grads[0], proj_in[0].T, proj_out[0].T, doc_starts, token_counts,
       queries.reshape(nqr * kkn, 128))
-    scores, grads = pl.pallas_call(
-        finish,
-        out_shape=(jax.ShapeDtypeStruct(scores.shape, f32), jax.ShapeDtypeStruct(grads.shape, f32)),
-        in_specs=[vmem, vmem],
-        out_specs=(vmem, vmem),
-    )(scores, grads)
     return scores.T, grads.reshape(docs, 1, share)
 
 

time: 23.6 us -> 22.4 us (0.949)
  Pallas kernels: 22.1 us -> 19.8 us
  local copies, waits for them, and re-layouts: 0 us -> 1.21 us
    pallas_call x1 -> x0, Pallas kernels: 1.38 us -> none  [shards(): pl.pallas_call(finish, out_shape=(jax.ShapeDtypeStruct(scores.shape, f32)...]
    unnamed x0 -> x2, local copies, waits for them, and re-layouts: none -> 1.21 us
    pallas_call x1, Pallas kernels: 20.7 us -> 19.8 us  [shards(): pl.pallas_call(functools.partial(kernel, g, width, chunks, docs), out_sha...]
where the time goes in v3:
time: 22.4 us; the launch traced here: 22.3 us
  Pallas kernels  19.8 us (88%)
  between operations  1.29 us (6%)
  local copies, waits for them, and re-layouts  1.21 us (5%)
    pallas_call x1, Pallas kernels, shards(): pl.pallas_call(functools.partial(kernel, g, width, chunks, docs), out_sha...  19.8 us
    unnamed x2, local copies, waits for them, and re-layouts  1.21 us

profile of v3, /device:TPU:0, one launch (start us, length us, event | category | flops | bytes accessed | tf_op | source)
XLA Modules:
  0.0 22.3 jit_solution(5966557666172687222)
XLA Ops:
  1.3 19.8 %shard_map.86 = (f32[4,256]{1,0:T(4,128)S(1)}, f32[64,128]{1,0:T(8,128)S(1)}) custom-call(bf16[384,14336]{1,0:T(8,128)(2,1)} %bitcast.13, bf16[384,4096]{1,0:T(8,128)(2,1)} %bitcast.14, bf16[64,14336]{1,0:T(8,128)(2,1)} %bitcast.15, bf16[64,4096]{1,0:T(8,128)(2,1)} %bitcast.16, s32[4]{0:T(128)} %starts_hbm.1, s32[1]{0:T(128)S(6)} %copy.14.counts_hbm, ...), custom_call_target="tpu_custom_call" | custom-call | tf_op jit(solution)/shard_map/pallas_call | solution.py:240
  21.0 0.6 %copy.12 = f32[256,4]{0,1:T(4,128)} copy(f32[256,4]{0,1:T(4,128)S(1)} %bitcast.12) | data formatting | bytes 8192
  21.6 0.6 %copy.13 = f32[4,1,2048]{2,1,0:T(1,128)} copy(f32[4,1,2048]{2,1,0:T(1,128)S(1)} %bitcast.11) | data formatting | bytes 65536

commit v4 on v3

--- a/solution.py
+++ b/solution.py
@@ -10,7 +10,7 @@
 
 MESH = pl.DeviceIdType.MESH
 NT = (((1,), (1,)), ((), ()))
-GREET_AT = 3
+GREET_AT = 2
 DOC_DIMS = (True, False, False)
 
 

time: 22.4 us -> 22.3 us (level)
  no operation moved by 1% of the time
where the time goes in v4:
time: 22.3 us; the launch traced here: 22.2 us
  Pallas kernels  19.7 us (88%)
  between operations  1.29 us (6%)
  local copies, waits for them, and re-layouts  1.21 us (5%)
    pallas_call x1, Pallas kernels, shards(): pl.pallas_call(functools.partial(kernel, g, width, chunks, docs), out_sha...  19.7 us
    unnamed x2, local copies, waits for them, and re-layouts  1.21 us

profile of v4, /device:TPU:0, one launch (start us, length us, event | category | flops | bytes accessed | tf_op | source)
XLA Modules:
  0.0 22.2 jit_solution(2420976530948052015)
XLA Ops:
  1.3 19.7 %shard_map.86 = (f32[4,256]{1,0:T(4,128)S(1)}, f32[64,128]{1,0:T(8,128)S(1)}) custom-call(bf16[384,14336]{1,0:T(8,128)(2,1)} %bitcast.13, bf16[384,4096]{1,0:T(8,128)(2,1)} %bitcast.14, bf16[64,14336]{1,0:T(8,128)(2,1)} %bitcast.15, bf16[64,4096]{1,0:T(8,128)(2,1)} %bitcast.16, s32[4]{0:T(128)} %starts_hbm.1, s32[1]{0:T(128)S(6)} %copy.14.counts_hbm, ...), custom_call_target="tpu_custom_call" | custom-call | tf_op jit(solution)/shard_map/pallas_call | solution.py:240
  21.0 0.6 %copy.12 = f32[256,4]{0,1:T(4,128)} copy(f32[256,4]{0,1:T(4,128)S(1)} %bitcast.12) | data formatting | bytes 8192
  21.6 0.6 %copy.13 = f32[4,1,2048]{2,1,0:T(1,128)} copy(f32[4,1,2048]{2,1,0:T(1,128)S(1)} %bitcast.11) | data formatting | bytes 65536
